TPU v7x, 32 devices: a whole 2x2x4 slice. The times are simulated.
32 devices in a mesh: inst: 4 (over z), shard: 8 (over y, x, core).
Axes of the slice: x: 2, y: 2, z: 4, core: 2. Of those that a mesh axis runs over, the one named last changes fastest.
Arguments:
- master_old: float32 [4, 16, 65536], P('inst', 'shard'), may hold values from -3 to 3
- first_old: float32 [4, 16, 65536], P('inst', 'shard'), may hold values from -2 to 2
- second_old: float32 [4, 16, 65536], P('inst', 'shard'), may hold values from 0.01 to 1
- healthy: int32 [8], replicated, may hold values from 0 to 3
- slice_table: int32 [16], replicated, may hold values from 0 to 15, as said below
Outputs:
- master_new: float32 [4, 16, 65536], P('inst', 'shard')
- first_new: float32 [4, 16, 65536], P('inst', 'shard')
- second_new: float32 [4, 16, 65536], P('inst', 'shard')
- params_half: bfloat16 [4, 16, 65536], P('inst', 'shard')
- checksum: float32 [4, 2], P('inst')
Inputs may be any that keep to these rules, and one draw needn't show every extreme that they name: slice_table[k] = (k + slice_table[0]) mod 16 for every k, with slice_table[0] odd and at least 3.
All inputs are finite; a program needn't handle non-finite values.
Results may differ from a plain program's by a relative error of at most 0.001.
Values sent between devices are 32-bit elements; how exact they have to be, the bound alone decides.
No kernel may reach another device: no remote copies, remote signals or barrier semaphores. Data moves between devices by JAX's collectives and lax.ppermute only.
A program may use at most 64 MiB of HBM per device.

v0:
```python
import jax
import jax.numpy as jnp
from jax import lax
from jax.sharding import PartitionSpec as P


def passed_along(value, axis, steps):
    count = lax.axis_size(axis)
    pairs = [(source, (source + steps) % count) for source in range(count)]
    return lax.ppermute(value, axis, pairs)


def from_root(block, axis, owner):
    block = jnp.where(lax.axis_index(axis) == owner, block, jnp.zeros_like(block))
    return lax.psum(block, axis)


def position_keys(flat_rows, columns):
    residue = flat_rows * (columns % 101) % 101
    offsets = jnp.arange(columns, dtype=jnp.int32)
    cycled = (residue[:, None] + offsets[None, :]) % 101
    return (cycled * 37 % 101 + 1).astype(jnp.float32) / 101.0


def weighted(master, first_moment, second, flat_rows):
    weights = position_keys(flat_rows, master.shape[2])
    combined = master[0] + first_moment[0] + second[0]
    return jnp.stack([jnp.sum(combined * weights), jnp.sum(master[0] * weights)])


def grand_total(partial_value):
    return lax.psum(partial_value, "shard")


def join_parts(pieces):
    return (
        lax.all_gather(pieces[0], "inst", axis=2, tiled=True),
        lax.all_gather(pieces[1], "inst", axis=2, tiled=True),
        lax.all_gather(pieces[2], "inst", axis=2, tiled=True),
    )


def reorder(arrays, rotation, owners):
    for bit_level in range((owners - 1).bit_length()):
        shifted = passed_along((arrays[0], arrays[1], arrays[2]), "shard", 1 << bit_level)
        chosen = rotation >> bit_level & 1 == 1
        arrays = tuple(
            (
                jnp.where(chosen, shifted_one, current)
                for shifted_one, current in zip(shifted, arrays)
            )
        )
    carried = passed_along((arrays[0][:, 1:2], arrays[1][:, 1:2], arrays[2][:, 1:2]), "shard", 1)
    return tuple(
        (
            jnp.concatenate([carried_one, current[:, 0:1]], axis=1)
            for carried_one, current in zip(carried, arrays)
        )
    )


def on_device(master_old, first_old, second_old, healthy, slice_table):
    source_index = lax.dynamic_index_in_dim(healthy, lax.axis_index("shard"), 0, keepdims=False)
    owners = lax.axis_size("shard")
    instances = lax.axis_size("inst")
    columns = master_old.shape[2]
    part_len = columns // instances
    normalizer = 1.0 / (2.0 * columns)
    rotation = slice_table[0] // 2
    master, first_moment, second = (
        from_root(master_old, "inst", source_index),
        from_root(first_old, "inst", source_index),
        from_root(second_old, "inst", source_index),
    )
    offset_start = lax.axis_index("inst") * part_len
    pieces = tuple(
        (
            lax.dynamic_slice_in_dim(stacked, offset_start, part_len, 2)
            for stacked in (master, first_moment, second)
        )
    )
    pieces = reorder(pieces, rotation, owners)
    master, first_moment, second = join_parts(pieces)
    new_rows = 2 * lax.axis_index("shard") + jnp.arange(2, dtype=jnp.int32)
    checksum = grand_total(weighted(master, first_moment, second, new_rows))
    checksum = jnp.reshape(checksum * normalizer, (1, 2))
    return (master, first_moment, second, master.astype(jnp.bfloat16), checksum)


def solution(mesh):
    placed = (
        P("inst", "shard", None),
        P("inst", "shard", None),
        P("inst", "shard", None),
        P(),
        P(),
    )
    return jax.shard_map(
        on_device,
        mesh=mesh,
        in_specs=placed,
        out_specs=(
            P("inst", "shard", None),
            P("inst", "shard", None),
            P("inst", "shard", None),
            P("inst", "shard", None),
            P("inst", None),
        ),
        check_vma=False,
    )
```

profile of v0, /device:TPU:0, one launch (start us, length us, event | category | flops | bytes accessed | tf_op | source)
XLA Modules:
  0.0 187.4 jit_solution(15723886663687752897)
XLA Ops:
  7.2 0.6 copy-done.4
  7.9 0.6 dynamic_slice.13
  9.1 2.1 %broadcast_select_fusion.2 = f32[1,2,65536]{2,1,0:T(2,128)} fusion(f32[1,2,65536]{2,1,0:T(2,128)} %param.5, pred[]{:T(512)S(6)} %eq.22), kind=kLoop, calls=%fused_computation.15 | loop fusion | flops 131072 | bytes 1048577 | tf_op jit(solution)/shard_map/jit(_where)/select_n | solution.py:14
  11.3 1.5 broadcast_select_fusion
  12.8 0.6 copy-done.3
  13.7 70.2 %all-reduce.3.cloned.1.call-done = (f32[1,2,65536]{2,1,0:T(2,128)}, f32[1,2,65536]{2,1,0:T(2,128)}, f32[1,2,65536]{2,1,0:T(2,128)}) async-done(((f32[1,2,65536]{2,1,0:T(2,128)}, f32[1,2,65536]{2,1,0:T(2,128)}, f32[1,2,65536]{2,1,0:T(2,128)}), (f32[1,2,65536]{2,1,0:T(2,128)}, f32[1,2,65536]{2,1,0:T(2,128)}, f32[1,2,65536]{2,1,0:T(2,128)})) %all-reduce.3.cloned.1.call-update) | async-done | bytes 1572880 | tf_op jit(solution)/shard_map/psum | solution.py:15
  83.9 1.0 constant_dynamic-slice_fusion
  84.9 0.9 constant_dynamic-slice_fusion.1
  85.8 1.6 collective-permute-start.4
  87.5 0.1 collective-permute-start
  87.6 2.6 %collective-permute-done.8 = f32[1,2,16384]{2,1,0:T(2,128)S(1)} collective-permute-done((f32[1,2,16384]{2,1,0:T(2,128)S(1)}, f32[1,2,16384]{2,1,0:T(2,128)S(1)}, u32[]{:S(2)}, u32[]{:S(2)}) %collective-permute-start.8) | collective-permute-done | bytes 131104 | tf_op jit(solution)/shard_map/ppermute | solution.py:10
  90.2 1.0 broadcast_select_fusion.3
  91.2 0.6 collective-permute-start.9
  91.8 1.0 broadcast_select_fusion.4
  92.8 2.4 %collective-permute-start.5 = (f32[1,2,16384]{2,1,0:T(2,128)S(1)}, f32[1,2,16384]{2,1,0:T(2,128)S(1)}, u32[]{:S(2)}, u32[]{:S(2)}) collective-permute-start(f32[1,2,16384]{2,1,0:T(2,128)S(1)} %broadcast_select_fusion.4), channel_id=1, source_target_pairs={{0,2},{1,3},{2,4},{3,5},{4,6},{5,7},{6,0},{7,1},{8,10},{9,11},{10,... | collective-permute-start | bytes 393224 | tf_op jit(solution)/shard_map/ppermute | solution.py:10
  95.2 0.1 broadcast_select_fusion.5
  95.3 0.6 collective-permute-start.1
  95.9 2.5 %collective-permute-done.9 = f32[1,2,16384]{2,1,0:T(2,128)S(1)} collective-permute-done((f32[1,2,16384]{2,1,0:T(2,128)S(1)}, f32[1,2,16384]{2,1,0:T(2,128)S(1)}, u32[]{:S(2)}, u32[]{:S(2)}) %collective-permute-start.9) | collective-permute-done | bytes 131104 | tf_op jit(solution)/shard_map/ppermute | solution.py:10
  98.4 0.1 broadcast_select_fusion.6
  98.5 1.7 collective-permute-start.10
  100.2 1.0 collective-permute-done.5
  101.2 0.1 broadcast_select_fusion.7
  101.3 1.0 collective-permute-start.6
  102.3 0.5 collective-permute-done.1
  102.8 0.1 broadcast_select_fusion.8
  102.9 0.8 collective-permute-start.2
  103.7 1.9 %collective-permute-done.10 = f32[1,2,16384]{2,1,0:T(2,128)S(1)} collective-permute-done((f32[1,2,16384]{2,1,0:T(2,128)S(1)}, f32[1,2,16384]{2,1,0:T(2,128)S(1)}, u32[]{:S(2)}, u32[]{:S(2)}) %collective-permute-start.10) | collective-permute-done | bytes 131104 | tf_op jit(solution)/shard_map/ppermute | solution.py:10
  105.6 0.1 broadcast_select_fusion.9
  105.7 0.1 fusion.8
  105.9 2.6 %collective-permute-done.6 = f32[1,2,16384]{2,1,0:T(2,128)S(1)} collective-permute-done((f32[1,2,16384]{2,1,0:T(2,128)S(1)}, f32[1,2,16384]{2,1,0:T(2,128)S(1)}, u32[]{:S(2)}, u32[]{:S(2)}) %collective-permute-start.6) | collective-permute-done | bytes 131104 | tf_op jit(solution)/shard_map/ppermute | solution.py:10
  108.4 0.1 broadcast_select_fusion.10
  108.5 0.1 fusion.9
  108.7 3.2 %collective-permute-done.2 = f32[1,2,16384]{2,1,0:T(2,128)S(1)} collective-permute-done((f32[1,2,16384]{2,1,0:T(2,128)S(1)}, f32[1,2,16384]{2,1,0:T(2,128)S(1)}, u32[]{:S(2)}, u32[]{:S(2)}) %collective-permute-start.2) | collective-permute-done | bytes 131104 | tf_op jit(solution)/shard_map/ppermute | solution.py:10
  111.9 0.1 fusion.10
  112.1 0.1 pad_maximum_fusion.2
  112.2 16.1 %all_gather.11 = f32[1,2,65536]{2,1,0:T(2,128)S(1)} all-gather(f32[1,2,16384]{2,1,0:T(2,128)S(1)} %pad_maximum_fusion.2), channel_id=1, replica_groups=mesh['inst'=4,'shard'=8] {'inst'}, dimensions={2}, use_global_device_ids=true | all-gather | bytes 655360 | tf_op jit(solution)/shard_map/all_gather | solution.py:39
  128.3 0.1 pad_maximum_fusion.1
  128.4 15.8 %all_gather.10 = f32[1,2,65536]{2,1,0:T(2,128)S(1)} all-gather(f32[1,2,16384]{2,1,0:T(2,128)S(1)} %pad_maximum_fusion.1), channel_id=1, replica_groups=mesh['inst'=4,'shard'=8] {'inst'}, dimensions={2}, use_global_device_ids=true | all-gather | bytes 655360 | tf_op jit(solution)/shard_map/all_gather | solution.py:38
  144.2 0.1 pad_maximum_fusion
  144.3 15.0 %all_gather.9 = f32[1,2,65536]{2,1,0:T(2,128)S(1)} all-gather(f32[1,2,16384]{2,1,0:T(2,128)S(1)} %pad_maximum_fusion), channel_id=1, replica_groups=mesh['inst'=4,'shard'=8] {'inst'}, dimensions={2}, use_global_device_ids=true | all-gather | bytes 655360 | tf_op jit(solution)/shard_map/all_gather | solution.py:37
  159.3 4.3 %fusion.6 = (f32[]{:T(128)}, f32[]{:T(128)}) fusion(f32[1,2,65536]{2,1,0:T(2,128)S(1)} %all_gather.11, f32[1,2,65536]{2,1,0:T(2,128)S(1)} %all_gather.10, f32[1,2,65536]{2,1,0:T(2,128)S(1)} %all_gather.9, s32[2]{0:T(128)S(1)} %and_select_fusion.2), kind=kLoop, calls=%fused_computation.9 | loop fusion | flops 3014654 | bytes 1572880 | tf_op jit(solution)/shard_map/reduce_sum | solution.py:28
  163.6 1.4 pad_maximum_fusion.3
  165.0 0.9 convert_element_type.6
  165.9 11.8 %psum.31 = f32[2]{0:T(128)S(1)} all-reduce(f32[2]{0:T(128)S(1)} %pad_maximum_fusion.3), channel_id=1, replica_groups=mesh['inst'=4,'shard'=8] {'shard'}, use_global_device_ids=true, to_apply=%region_5.6 | all-reduce | flops 2 | bytes 16 | tf_op jit(solution)/shard_map/psum | solution.py:32
  177.6 0.5 multiply_bitcast_fusion
  178.1 0.8 copy.16
  178.9 0.8 copy.17
  179.7 0.8 copy.18
  (22 shorter events, 0.4 us)
Async XLA Ops:
  7.2 76.7 %all-reduce.3.cloned.1.call-start = ((), (), s32[]{:S(2)}) async-start(), calls=%async_computation | async-start | bytes 3145728 | tf_op jit(solution)/shard_map/psum | solution.py:15
  7.2 0.7 copy-start.4
  9.1 2.2 %copy-start = (f32[1,2,65536]{2,1,0:T(2,128)S(1)}, f32[1,2,65536]{2,1,0:T(2,128)}, u32[]{:S(2)}) copy-start(f32[1,2,65536]{2,1,0:T(2,128)} %param.7) | copy-start | bytes 1572868
  9.1 2.2 %copy-start.1 = (f32[1,2,65536]{2,1,0:T(2,128)S(1)}, f32[1,2,65536]{2,1,0:T(2,128)}, u32[]{:S(2)}) copy-start(f32[1,2,65536]{2,1,0:T(2,128)} %param.6) | copy-start | bytes 1572868
  12.8 0.7 copy-start.3
  83.9 3.6 %copy-start.2 = (f32[1,2,65536]{2,1,0:T(2,128)S(1)}, f32[1,2,65536]{2,1,0:T(2,128)}, u32[]{:S(2)}) copy-start(f32[1,2,65536]{2,1,0:T(2,128)} %get-tuple-element.7) | copy-start | bytes 1572868
  84.9 5.3 %collective-permute-start.8 = (f32[1,2,16384]{2,1,0:T(2,128)S(1)}, f32[1,2,16384]{2,1,0:T(2,128)S(1)}, u32[]{:S(2)}, u32[]{:S(2)}) collective-permute-start(f32[1,2,16384]{2,1,0:T(2,128)S(1)} %constant_dynamic-slice_fusion), channel_id=1, source_target_pairs={{0,1},{1,2},{2,3},{3,4},{4,5},{5,6},{6,7},{7,0},{8,9},{9,10},{10,1... | collective-permute-start | bytes 393224 | tf_op jit(solution)/shard_map/ppermute | solution.py:10
  85.8 6.0 %collective-permute-start.4 = (f32[1,2,16384]{2,1,0:T(2,128)S(1)}, f32[1,2,16384]{2,1,0:T(2,128)S(1)}, u32[]{:S(2)}, u32[]{:S(2)}) collective-permute-start(f32[1,2,16384]{2,1,0:T(2,128)S(1)} %constant_dynamic-slice_fusion.1), channel_id=1, source_target_pairs={{0,1},{1,2},{2,3},{3,4},{4,5},{5,6},{6,7},{7,0},{8,9},{9,10},{10,1... | collective-permute-start | bytes 393224 | tf_op jit(solution)/shard_map/ppermute | solution.py:10
  87.5 7.7 %collective-permute-start = (f32[1,2,16384]{2,1,0:T(2,128)S(1)}, f32[1,2,16384]{2,1,0:T(2,128)S(1)}, u32[]{:S(2)}, u32[]{:S(2)}) collective-permute-start(f32[1,2,16384]{2,1,0:T(2,128)S(1)} %constant_dynamic-slice_fusion.2), channel_id=1, source_target_pairs={{0,1},{1,2},{2,3},{3,4},{4,5},{5,6},{6,7},{7,0},{8,9},{9,10},{10,1... | collective-permute-start | bytes 393224 | tf_op jit(solution)/shard_map/ppermute | solution.py:10
  91.2 7.2 %collective-permute-start.9 = (f32[1,2,16384]{2,1,0:T(2,128)S(1)}, f32[1,2,16384]{2,1,0:T(2,128)S(1)}, u32[]{:S(2)}, u32[]{:S(2)}) collective-permute-start(f32[1,2,16384]{2,1,0:T(2,128)S(1)} %broadcast_select_fusion.3), channel_id=1, source_target_pairs={{0,2},{1,3},{2,4},{3,5},{4,6},{5,7},{6,0},{7,1},{8,10},{9,11},{10,... | collective-permute-start | bytes 393224 | tf_op jit(solution)/shard_map/ppermute | solution.py:10
  92.8 8.5 %collective-permute-start.5 = (f32[1,2,16384]{2,1,0:T(2,128)S(1)}, f32[1,2,16384]{2,1,0:T(2,128)S(1)}, u32[]{:S(2)}, u32[]{:S(2)}) collective-permute-start(f32[1,2,16384]{2,1,0:T(2,128)S(1)} %broadcast_select_fusion.4), channel_id=1, source_target_pairs={{0,2},{1,3},{2,4},{3,5},{4,6},{5,7},{6,0},{7,1},{8,10},{9,11},{10,... | collective-permute-start | bytes 393224 | tf_op jit(solution)/shard_map/ppermute | solution.py:10
  95.3 7.5 %collective-permute-start.1 = (f32[1,2,16384]{2,1,0:T(2,128)S(1)}, f32[1,2,16384]{2,1,0:T(2,128)S(1)}, u32[]{:S(2)}, u32[]{:S(2)}) collective-permute-start(f32[1,2,16384]{2,1,0:T(2,128)S(1)} %broadcast_select_fusion.5), channel_id=1, source_target_pairs={{0,2},{1,3},{2,4},{3,5},{4,6},{5,7},{6,0},{7,1},{8,10},{9,11},{10,... | collective-permute-start | bytes 393224 | tf_op jit(solution)/shard_map/ppermute | solution.py:10
  98.5 7.1 %collective-permute-start.10 = (f32[1,2,16384]{2,1,0:T(2,128)S(1)}, f32[1,2,16384]{2,1,0:T(2,128)S(1)}, u32[]{:S(2)}, u32[]{:S(2)}) collective-permute-start(f32[1,2,16384]{2,1,0:T(2,128)S(1)} %broadcast_select_fusion.6), channel_id=1, source_target_pairs={{0,4},{1,5},{2,6},{3,7},{4,0},{5,1},{6,2},{7,3},{8,12},{9,13},{10,... | collective-permute-start | bytes 393224 | tf_op jit(solution)/shard_map/ppermute | solution.py:10
  101.3 7.1 %collective-permute-start.6 = (f32[1,2,16384]{2,1,0:T(2,128)S(1)}, f32[1,2,16384]{2,1,0:T(2,128)S(1)}, u32[]{:S(2)}, u32[]{:S(2)}) collective-permute-start(f32[1,2,16384]{2,1,0:T(2,128)S(1)} %broadcast_select_fusion.7), channel_id=1, source_target_pairs={{0,4},{1,5},{2,6},{3,7},{4,0},{5,1},{6,2},{7,3},{8,12},{9,13},{10,... | collective-permute-start | bytes 393224 | tf_op jit(solution)/shard_map/ppermute | solution.py:10
  102.9 9.0 %collective-permute-start.2 = (f32[1,2,16384]{2,1,0:T(2,128)S(1)}, f32[1,2,16384]{2,1,0:T(2,128)S(1)}, u32[]{:S(2)}, u32[]{:S(2)}) collective-permute-start(f32[1,2,16384]{2,1,0:T(2,128)S(1)} %broadcast_select_fusion.8), channel_id=1, source_target_pairs={{0,4},{1,5},{2,6},{3,7},{4,0},{5,1},{6,2},{7,3},{8,12},{9,13},{10,... | collective-permute-start | bytes 393224 | tf_op jit(solution)/shard_map/ppermute | solution.py:10
  105.8 6.3 %collective-permute-start.11 = (f32[1,1,16384]{2,1,0:T(1,128)S(1)}, f32[1,1,16384]{2,1,0:T(1,128)S(1)}, u32[]{:S(2)}, u32[]{:S(2)}) collective-permute-start(f32[1,1,16384]{2,1,0:T(1,128)S(1)} %get-tuple-element.10), channel_id=1, source_target_pairs={{0,1},{1,2},{2,3},{3,4},{4,5},{5,6},{6,7},{7,0},{8,9},{9,10},{10,1... | collective-permute-start | bytes 196616 | tf_op jit(solution)/shard_map/ppermute | solution.py:10
  108.6 19.7 %collective-permute-start.7 = (f32[1,1,16384]{2,1,0:T(1,128)S(1)}, f32[1,1,16384]{2,1,0:T(1,128)S(1)}, u32[]{:S(2)}, u32[]{:S(2)}) collective-permute-start(f32[1,1,16384]{2,1,0:T(1,128)S(1)} %get-tuple-element.12), channel_id=1, source_target_pairs={{0,1},{1,2},{2,3},{3,4},{4,5},{5,6},{6,7},{7,0},{8,9},{9,10},{10,1... | collective-permute-start | bytes 196616 | tf_op jit(solution)/shard_map/ppermute | solution.py:10
  112.0 32.2 %collective-permute-start.3 = (f32[1,1,16384]{2,1,0:T(1,128)S(1)}, f32[1,1,16384]{2,1,0:T(1,128)S(1)}, u32[]{:S(2)}, u32[]{:S(2)}) collective-permute-start(f32[1,1,16384]{2,1,0:T(1,128)S(1)} %get-tuple-element.14), channel_id=1, source_target_pairs={{0,1},{1,2},{2,3},{3,4},{4,5},{5,6},{6,7},{7,0},{8,9},{9,10},{10,1... | collective-permute-start | bytes 196616 | tf_op jit(solution)/shard_map/ppermute | solution.py:10
Sparse Core Ops, SparseCore 0:
  12.9 70.8 all-reduce.2
where the time goes:
time: 188 us; the launch traced here: 187 us
  waiting for transfers between devices  84.6 us (45%)
  blocking collectives  58.6 us (31%)
  between operations  15 us (8%)
  other arithmetic  13.5 us (7%)
  starting transfers between devices  9.11 us (5%)
  local copies, waits for them, and re-layouts  6.49 us (3%)
    psum x1, waiting for transfers between devices, from_root(): return lax.psum(block, axis)  70.2 us
    all_gather x1, blocking collectives, join_parts(): lax.all_gather(pieces[2], 'inst', axis=2, tiled=True)  16.1 us
    all_gather x1, blocking collectives, join_parts(): lax.all_gather(pieces[1], 'inst', axis=2, tiled=True)  15.8 us
    all_gather x1, blocking collectives, join_parts(): lax.all_gather(pieces[0], 'inst', axis=2, tiled=True)  15 us
    ppermute x12, waiting for transfers between devices, passed_along(): return lax.ppermute(value, axis, pairs)  14.4 us
    psum x1, blocking collectives, grand_total(): return lax.psum(partial_value, 'shard')  11.8 us
    ppermute x12, starting transfers between devices, passed_along(): return lax.ppermute(value, axis, pairs)  9.07 us
    reduce_sum x1, other arithmetic, weighted(): jnp.sum(combined * weights)  4.28 us
  transfers between devices with their start and end apart: 13, of which 8 were waited for; matrix products, arithmetic and copies ran while one was open for 2% of the time, Pallas kernels for 0%

commit v1 on v0

--- a/solution.py
+++ b/solution.py
@@ -2,6 +2,23 @@
 import jax.numpy as jnp
 from jax import lax
 from jax.sharding import PartitionSpec as P
+
+
+def carry_edge(packet, d0):
+    earlier = list(packet.shape[1:])
+    earlier[d0] *= packet.shape[0]
+    return jnp.moveaxis(packet, 0, d0).reshape(earlier)
+
+
+def wait_point(arr, axis_id, along_dim):
+    n = lax.axis_size(axis_id)
+    xs_all = [arr]
+    buffers = tuple(((jj, (jj + 1) % n) for jj in range(n)))
+    while len(xs_all) < n:
+        xs_all.append(lax.ppermute(xs_all[-1], axis_id, buffers))
+    new = lax.axis_index(axis_id)
+    xs_all = jnp.stack(xs_all)[(new - jnp.arange(n)) % n]
+    return carry_edge(xs_all, along_dim)
 
 
 def passed_along(value, axis, steps):
@@ -34,7 +51,7 @@
 
 def join_parts(pieces):
     return (
-        lax.all_gather(pieces[0], "inst", axis=2, tiled=True),
+        wait_point(pieces[0], "inst", 2),
         lax.all_gather(pieces[1], "inst", axis=2, tiled=True),
         lax.all_gather(pieces[2], "inst", axis=2, tiled=True),
     )

time: 188 us -> 187 us (level)
  blocking collectives: 58.6 us -> 45.3 us
  waiting for transfers between devices: 84.6 us -> 90.7 us
  other arithmetic: 13.5 us -> 17.5 us
  starting transfers between devices: 9.11 us -> 11.2 us
    all_gather x1 -> x0, blocking collectives: 15 us -> none  [join_parts(): lax.all_gather(pieces[0], 'inst', axis=2, tiled=True)]
    reduce_sum x0 -> x1, other arithmetic: none -> 3.9 us  [weighted(): jnp.sum(master[0] * weights)]
    ppermute x12, waiting for transfers between devices: 14.4 us -> 17.8 us  [passed_along(): return lax.ppermute(value, axis, pairs)]
    ppermute x0 -> x3, waiting for transfers between devices: none -> 2.73 us  [wait_point(): xs_all.append(lax.ppermute(xs_all[-1], axis_id, buffers))]
    ppermute x0 -> x3, starting transfers between devices: none -> 2.06 us  [wait_point(): xs_all.append(lax.ppermute(xs_all[-1], axis_id, buffers))]
  transfers between devices with their start and end apart: 13 -> 16, of which waited for: 8 -> 11; matrix products, arithmetic and copies ran while one was open for 2% -> 2% of each run, Pallas kernels for 0% -> 0%
where the time goes in v1:
time: 187 us
  waiting for transfers between devices  90.7 us (49%)
  blocking collectives  45.3 us (24%)
  other arithmetic  17.5 us (9%)
  between operations  15.1 us (8%)
  starting transfers between devices  11.2 us (6%)
  local copies, waits for them, and re-layouts  6.81 us (4%)
    psum x1, waiting for transfers between devices, from_root(): return lax.psum(block, axis)  70.1 us
    ppermute x12, waiting for transfers between devices, passed_along(): return lax.ppermute(value, axis, pairs)  17.8 us
    all_gather x1, blocking collectives, join_parts(): lax.all_gather(pieces[1], 'inst', axis=2, tiled=True)  17.2 us
    all_gather x1, blocking collectives, join_parts(): lax.all_gather(pieces[2], 'inst', axis=2, tiled=True)  16.3 us
    psum x1, blocking collectives, grand_total(): return lax.psum(partial_value, 'shard')  11.8 us
    ppermute x12, starting transfers between devices, passed_along(): return lax.ppermute(value, axis, pairs)  9.07 us
    reduce_sum x1, other arithmetic, weighted(): jnp.sum(combined * weights)  4.08 us
    reduce_sum x1, other arithmetic, weighted(): jnp.sum(master[0] * weights)  3.9 us
  transfers between devices with their start and end apart: 16, of which 11 were waited for; matrix products, arithmetic and copies ran while one was open for 2% of the time, Pallas kernels for 0%

profile of v1, /device:TPU:0, one launch (start us, length us, event | category | flops | bytes accessed | tf_op | source)
XLA Modules:
  0.0 186.5 jit_solution(12155491193941504130)
XLA Ops:
  7.2 0.6 copy-done.5
  7.9 0.6 dynamic_slice.13
  9.1 2.2 %broadcast_select_fusion.2 = f32[1,2,65536]{2,1,0:T(2,128)} fusion(f32[1,2,65536]{2,1,0:T(2,128)} %param.5, pred[]{:T(512)S(6)} %eq.24), kind=kLoop, calls=%fused_computation.23 | loop fusion | flops 131072 | bytes 1048577 | tf_op jit(solution)/shard_map/jit(_where)/select_n | solution.py:31
  11.3 1.5 broadcast_select_fusion
  12.8 0.6 copy-done.4
  13.8 70.1 %all-reduce.3.cloned.1.call-done = (f32[1,2,65536]{2,1,0:T(2,128)}, f32[1,2,65536]{2,1,0:T(2,128)}, f32[1,2,65536]{2,1,0:T(2,128)}) async-done(((f32[1,2,65536]{2,1,0:T(2,128)}, f32[1,2,65536]{2,1,0:T(2,128)}, f32[1,2,65536]{2,1,0:T(2,128)}), (f32[1,2,65536]{2,1,0:T(2,128)}, f32[1,2,65536]{2,1,0:T(2,128)}, f32[1,2,65536]{2,1,0:T(2,128)})) %all-reduce.3.cloned.1.call-update) | async-done | bytes 1572880 | tf_op jit(solution)/shard_map/psum | solution.py:32
  83.9 1.0 constant_dynamic-slice_fusion.2
  84.9 0.9 constant_dynamic-slice_fusion.1
  85.8 1.6 collective-permute-start.7
  87.5 0.1 collective-permute-start.11
  87.6 2.6 %collective-permute-done = f32[1,2,16384]{2,1,0:T(2,128)S(1)} collective-permute-done((f32[1,2,16384]{2,1,0:T(2,128)S(1)}, f32[1,2,16384]{2,1,0:T(2,128)S(1)}, u32[]{:S(2)}, u32[]{:S(2)}) %collective-permute-start) | collective-permute-done | bytes 131104 | tf_op jit(solution)/shard_map/ppermute | solution.py:27
  90.2 1.0 broadcast_select_fusion.5
  91.2 0.6 collective-permute-start.1
  91.8 1.0 broadcast_select_fusion.4
  92.8 2.4 %collective-permute-start.8 = (f32[1,2,16384]{2,1,0:T(2,128)S(1)}, f32[1,2,16384]{2,1,0:T(2,128)S(1)}, u32[]{:S(2)}, u32[]{:S(2)}) collective-permute-start(f32[1,2,16384]{2,1,0:T(2,128)S(1)} %broadcast_select_fusion.4), channel_id=1, source_target_pairs={{0,2},{1,3},{2,4},{3,5},{4,6},{5,7},{6,0},{7,1},{8,10},{9,11},{10,... | collective-permute-start | bytes 393224 | tf_op jit(solution)/shard_map/ppermute | solution.py:27
  95.3 0.6 collective-permute-start.12
  95.9 2.5 %collective-permute-done.1 = f32[1,2,16384]{2,1,0:T(2,128)S(1)} collective-permute-done((f32[1,2,16384]{2,1,0:T(2,128)S(1)}, f32[1,2,16384]{2,1,0:T(2,128)S(1)}, u32[]{:S(2)}, u32[]{:S(2)}) %collective-permute-start.1) | collective-permute-done | bytes 131104 | tf_op jit(solution)/shard_map/ppermute | solution.py:27
  98.5 1.7 collective-permute-start.2
  100.2 1.0 collective-permute-done.8
  101.3 1.0 collective-permute-start.9
  102.3 0.5 collective-permute-done.12
  102.9 0.8 collective-permute-start.13
  103.7 1.9 %collective-permute-done.2 = f32[1,2,16384]{2,1,0:T(2,128)S(1)} collective-permute-done((f32[1,2,16384]{2,1,0:T(2,128)S(1)}, f32[1,2,16384]{2,1,0:T(2,128)S(1)}, u32[]{:S(2)}, u32[]{:S(2)}) %collective-permute-start.2) | collective-permute-done | bytes 131104 | tf_op jit(solution)/shard_map/ppermute | solution.py:27
  105.7 0.1 fusion.19
  105.9 2.6 %collective-permute-done.9 = f32[1,2,16384]{2,1,0:T(2,128)S(1)} collective-permute-done((f32[1,2,16384]{2,1,0:T(2,128)S(1)}, f32[1,2,16384]{2,1,0:T(2,128)S(1)}, u32[]{:S(2)}, u32[]{:S(2)}) %collective-permute-start.9) | collective-permute-done | bytes 131104 | tf_op jit(solution)/shard_map/ppermute | solution.py:27
  108.5 0.1 fusion.18
  108.7 3.2 %collective-permute-done.13 = f32[1,2,16384]{2,1,0:T(2,128)S(1)} collective-permute-done((f32[1,2,16384]{2,1,0:T(2,128)S(1)}, f32[1,2,16384]{2,1,0:T(2,128)S(1)}, u32[]{:S(2)}, u32[]{:S(2)}) %collective-permute-start.13) | collective-permute-done | bytes 131104 | tf_op jit(solution)/shard_map/ppermute | solution.py:27
  111.9 0.1 fusion.17
  112.1 0.1 fusion.16
  112.3 0.9 collective-permute-start.4
  113.1 0.1 collective-permute-done.10
  113.3 0.1 pad_maximum_fusion.1
  113.4 3.3 %collective-permute-done.14 = f32[1,1,16384]{2,1,0:T(1,128)S(1)} collective-permute-done((f32[1,1,16384]{2,1,0:T(1,128)S(1)}, f32[1,1,16384]{2,1,0:T(1,128)S(1)}, u32[]{:S(2)}, u32[]{:S(2)}) %collective-permute-start.14) | collective-permute-done | bytes 65568 | tf_op jit(solution)/shard_map/ppermute | solution.py:27
  116.7 0.1 pad_maximum_fusion.2
  116.8 2.7 %collective-permute-done.4 = f32[1,2,16384]{2,1,0:T(2,128)S(1)} collective-permute-done((f32[1,2,16384]{2,1,0:T(2,128)S(1)}, f32[1,2,16384]{2,1,0:T(2,128)S(1)}, u32[]{:S(2)}, u32[]{:S(2)}) %collective-permute-start.4) | collective-permute-done | bytes 131104 | tf_op jit(solution)/shard_map/ppermute | solution.py:18
  119.5 17.2 %all_gather.6 = f32[1,2,65536]{2,1,0:T(2,128)S(1)} all-gather(f32[1,2,16384]{2,1,0:T(2,128)S(1)} %pad_maximum_fusion.1), channel_id=1, replica_groups=mesh['inst'=4,'shard'=8] {'inst'}, dimensions={2}, use_global_device_ids=true | all-gather | bytes 655360 | tf_op jit(solution)/shard_map/all_gather | solution.py:55
  136.8 1.2 collective-permute-start.6
  138.0 16.3 %all_gather.7 = f32[1,2,65536]{2,1,0:T(2,128)S(1)} all-gather(f32[1,2,16384]{2,1,0:T(2,128)S(1)} %pad_maximum_fusion.2), channel_id=1, replica_groups=mesh['inst'=4,'shard'=8] {'inst'}, dimensions={2}, use_global_device_ids=true | all-gather | bytes 655360 | tf_op jit(solution)/shard_map/all_gather | solution.py:56
  154.2 0.2 maximum_bitcast_fusion
  154.5 1.1 gather_fusion
  155.6 3.9 %fusion.12 = f32[]{:T(128)} fusion(f32[4,2,16384]{2,1,0:T(2,128)S(1)} %gather_fusion, s32[4,16384]{1,0:T(4,128)S(1)} %multiply_add_fusion, s32[2]{0:T(128)S(1)} %and_select_fusion.4), kind=kLoop, calls=%fused_computation.20 | loop fusion | flops 2490367 | bytes 786444 | tf_op jit(solution)/shard_map/reduce_sum | solution.py:45
  159.5 4.1 %fusion.13 = f32[]{:T(128)} fusion(f32[1,2,65536]{2,1,0:T(2,128)S(1)} %all_gather.7, f32[2,65536]{1,0:T(2,128)S(1)} %bitcast.38, f32[1,2,65536]{2,1,0:T(2,128)S(1)} %all_gather.6, s32[2]{0:T(128)S(1)} %and_select_fusion.4), kind=kLoop, calls=%fused_computation.24 | loop fusion | flops 2752511 | bytes 1572876 | tf_op jit(solution)/shard_map/reduce_sum | solution.py:45
  163.6 1.4 pad_maximum_fusion.3
  164.9 0.9 convert_element_type.23
  165.8 11.8 %psum.31 = f32[2]{0:T(128)S(1)} all-reduce(f32[2]{0:T(128)S(1)} %pad_maximum_fusion.3), channel_id=1, replica_groups=mesh['inst'=4,'shard'=8] {'shard'}, use_global_device_ids=true, to_apply=%region_5.6 | all-reduce | flops 2 | bytes 16 | tf_op jit(solution)/shard_map/psum | solution.py:49
  177.6 0.5 multiply_bitcast_fusion
  178.1 0.8 copy.15
  178.9 0.8 copy.16
  (34 shorter events, 0.9 us)
Async XLA Ops:
  7.2 76.7 %all-reduce.3.cloned.1.call-start = ((), (), s32[]{:S(2)}) async-start(), calls=%async_computation | async-start | bytes 3145728 | tf_op jit(solution)/shard_map/psum | solution.py:32
  7.2 0.7 copy-start.5
  9.1 2.2 %copy-start.1 = (f32[1,2,65536]{2,1,0:T(2,128)S(1)}, f32[1,2,65536]{2,1,0:T(2,128)}, u32[]{:S(2)}) copy-start(f32[1,2,65536]{2,1,0:T(2,128)} %param.7) | copy-start | bytes 1572868
  9.1 2.2 %copy-start.2 = (f32[1,2,65536]{2,1,0:T(2,128)S(1)}, f32[1,2,65536]{2,1,0:T(2,128)}, u32[]{:S(2)}) copy-start(f32[1,2,65536]{2,1,0:T(2,128)} %param.6) | copy-start | bytes 1572868
  12.8 0.7 copy-start.4
  83.9 3.6 %copy-start.3 = (f32[1,2,65536]{2,1,0:T(2,128)S(1)}, f32[1,2,65536]{2,1,0:T(2,128)}, u32[]{:S(2)}) copy-start(f32[1,2,65536]{2,1,0:T(2,128)} %get-tuple-element.7) | copy-start | bytes 1572868
  84.9 5.3 %collective-permute-start = (f32[1,2,16384]{2,1,0:T(2,128)S(1)}, f32[1,2,16384]{2,1,0:T(2,128)S(1)}, u32[]{:S(2)}, u32[]{:S(2)}) collective-permute-start(f32[1,2,16384]{2,1,0:T(2,128)S(1)} %constant_dynamic-slice_fusion.2), channel_id=1, source_target_pairs={{0,1},{1,2},{2,3},{3,4},{4,5},{5,6},{6,7},{7,0},{8,9},{9,10},{10,1... | collective-permute-start | bytes 393224 | tf_op jit(solution)/shard_map/ppermute | solution.py:27
  85.8 6.0 %collective-permute-start.7 = (f32[1,2,16384]{2,1,0:T(2,128)S(1)}, f32[1,2,16384]{2,1,0:T(2,128)S(1)}, u32[]{:S(2)}, u32[]{:S(2)}) collective-permute-start(f32[1,2,16384]{2,1,0:T(2,128)S(1)} %constant_dynamic-slice_fusion.1), channel_id=1, source_target_pairs={{0,1},{1,2},{2,3},{3,4},{4,5},{5,6},{6,7},{7,0},{8,9},{9,10},{10,1... | collective-permute-start | bytes 393224 | tf_op jit(solution)/shard_map/ppermute | solution.py:27
  87.5 7.7 %collective-permute-start.11 = (f32[1,2,16384]{2,1,0:T(2,128)S(1)}, f32[1,2,16384]{2,1,0:T(2,128)S(1)}, u32[]{:S(2)}, u32[]{:S(2)}) collective-permute-start(f32[1,2,16384]{2,1,0:T(2,128)S(1)} %constant_dynamic-slice_fusion), channel_id=1, source_target_pairs={{0,1},{1,2},{2,3},{3,4},{4,5},{5,6},{6,7},{7,0},{8,9},{9,10},{10,1... | collective-permute-start | bytes 393224 | tf_op jit(solution)/shard_map/ppermute | solution.py:27
  91.2 7.2 %collective-permute-start.1 = (f32[1,2,16384]{2,1,0:T(2,128)S(1)}, f32[1,2,16384]{2,1,0:T(2,128)S(1)}, u32[]{:S(2)}, u32[]{:S(2)}) collective-permute-start(f32[1,2,16384]{2,1,0:T(2,128)S(1)} %broadcast_select_fusion.5), channel_id=1, source_target_pairs={{0,2},{1,3},{2,4},{3,5},{4,6},{5,7},{6,0},{7,1},{8,10},{9,11},{10,... | collective-permute-start | bytes 393224 | tf_op jit(solution)/shard_map/ppermute | solution.py:27
  92.8 8.5 %collective-permute-start.8 = (f32[1,2,16384]{2,1,0:T(2,128)S(1)}, f32[1,2,16384]{2,1,0:T(2,128)S(1)}, u32[]{:S(2)}, u32[]{:S(2)}) collective-permute-start(f32[1,2,16384]{2,1,0:T(2,128)S(1)} %broadcast_select_fusion.4), channel_id=1, source_target_pairs={{0,2},{1,3},{2,4},{3,5},{4,6},{5,7},{6,0},{7,1},{8,10},{9,11},{10,... | collective-permute-start | bytes 393224 | tf_op jit(solution)/shard_map/ppermute | solution.py:27
  95.3 7.5 %collective-permute-start.12 = (f32[1,2,16384]{2,1,0:T(2,128)S(1)}, f32[1,2,16384]{2,1,0:T(2,128)S(1)}, u32[]{:S(2)}, u32[]{:S(2)}) collective-permute-start(f32[1,2,16384]{2,1,0:T(2,128)S(1)} %broadcast_select_fusion.3), channel_id=1, source_target_pairs={{0,2},{1,3},{2,4},{3,5},{4,6},{5,7},{6,0},{7,1},{8,10},{9,11},{10,... | collective-permute-start | bytes 393224 | tf_op jit(solution)/shard_map/ppermute | solution.py:27
  98.5 7.1 %collective-permute-start.2 = (f32[1,2,16384]{2,1,0:T(2,128)S(1)}, f32[1,2,16384]{2,1,0:T(2,128)S(1)}, u32[]{:S(2)}, u32[]{:S(2)}) collective-permute-start(f32[1,2,16384]{2,1,0:T(2,128)S(1)} %broadcast_select_fusion.8), channel_id=1, source_target_pairs={{0,4},{1,5},{2,6},{3,7},{4,0},{5,1},{6,2},{7,3},{8,12},{9,13},{10,... | collective-permute-start | bytes 393224 | tf_op jit(solution)/shard_map/ppermute | solution.py:27
  101.3 7.1 %collective-permute-start.9 = (f32[1,2,16384]{2,1,0:T(2,128)S(1)}, f32[1,2,16384]{2,1,0:T(2,128)S(1)}, u32[]{:S(2)}, u32[]{:S(2)}) collective-permute-start(f32[1,2,16384]{2,1,0:T(2,128)S(1)} %broadcast_select_fusion.7), channel_id=1, source_target_pairs={{0,4},{1,5},{2,6},{3,7},{4,0},{5,1},{6,2},{7,3},{8,12},{9,13},{10,... | collective-permute-start | bytes 393224 | tf_op jit(solution)/shard_map/ppermute | solution.py:27
  102.9 9.0 %collective-permute-start.13 = (f32[1,2,16384]{2,1,0:T(2,128)S(1)}, f32[1,2,16384]{2,1,0:T(2,128)S(1)}, u32[]{:S(2)}, u32[]{:S(2)}) collective-permute-start(f32[1,2,16384]{2,1,0:T(2,128)S(1)} %broadcast_select_fusion.6), channel_id=1, source_target_pairs={{0,4},{1,5},{2,6},{3,7},{4,0},{5,1},{6,2},{7,3},{8,12},{9,13},{10,... | collective-permute-start | bytes 393224 | tf_op jit(solution)/shard_map/ppermute | solution.py:27
  105.8 6.3 %collective-permute-start.3 = (f32[1,1,16384]{2,1,0:T(1,128)S(1)}, f32[1,1,16384]{2,1,0:T(1,128)S(1)}, u32[]{:S(2)}, u32[]{:S(2)}) collective-permute-start(f32[1,1,16384]{2,1,0:T(1,128)S(1)} %get-tuple-element.14), channel_id=1, source_target_pairs={{0,1},{1,2},{2,3},{3,4},{4,5},{5,6},{6,7},{7,0},{8,9},{9,10},{10,1... | collective-permute-start | bytes 196616 | tf_op jit(solution)/shard_map/ppermute | solution.py:27
  108.6 4.6 %collective-permute-start.10 = (f32[1,1,16384]{2,1,0:T(1,128)S(1)}, f32[1,1,16384]{2,1,0:T(1,128)S(1)}, u32[]{:S(2)}, u32[]{:S(2)}) collective-permute-start(f32[1,1,16384]{2,1,0:T(1,128)S(1)} %get-tuple-element.10), channel_id=1, source_target_pairs={{0,1},{1,2},{2,3},{3,4},{4,5},{5,6},{6,7},{7,0},{8,9},{9,10},{10,1... | collective-permute-start | bytes 196616 | tf_op jit(solution)/shard_map/ppermute | solution.py:27
  112.0 4.6 %collective-permute-start.14 = (f32[1,1,16384]{2,1,0:T(1,128)S(1)}, f32[1,1,16384]{2,1,0:T(1,128)S(1)}, u32[]{:S(2)}, u32[]{:S(2)}) collective-permute-start(f32[1,1,16384]{2,1,0:T(1,128)S(1)} %get-tuple-element.8), channel_id=1, source_target_pairs={{0,1},{1,2},{2,3},{3,4},{4,5},{5,6},{6,7},{7,0},{8,9},{9,10},{10,1... | collective-permute-start | bytes 196616 | tf_op jit(solution)/shard_map/ppermute | solution.py:27
  112.3 7.3 %collective-permute-start.4 = (f32[1,2,16384]{2,1,0:T(2,128)S(1)}, f32[1,2,16384]{2,1,0:T(2,128)S(1)}, u32[]{:S(2)}, u32[]{:S(2)}) collective-permute-start(f32[1,2,16384]{2,1,0:T(2,128)S(1)} %get-tuple-element.13), channel_id=1, source_target_pairs={{0,8},{8,16},{16,24},{24,0},{1,9},{9,17},{17,25},{25,1},{2,10},{10... | collective-permute-start | bytes 393224 | tf_op jit(solution)/shard_map/ppermute | solution.py:18
  119.5 17.2 %collective-permute-start.5 = (f32[1,2,16384]{2,1,0:T(2,128)S(1)}, f32[1,2,16384]{2,1,0:T(2,128)S(1)}, u32[]{:S(2)}, u32[]{:S(2)}) collective-permute-start(f32[1,2,16384]{2,1,0:T(2,128)S(1)} %collective-permute-done.4), channel_id=1, source_target_pairs={{0,8},{8,16},{16,24},{24,0},{1,9},{9,17},{17,25},{25,1},{2,10},{10... | collective-permute-start | bytes 393224 | tf_op jit(solution)/shard_map/ppermute | solution.py:18
  136.8 17.5 %collective-permute-start.6 = (f32[1,2,16384]{2,1,0:T(2,128)S(1)}, f32[1,2,16384]{2,1,0:T(2,128)S(1)}, u32[]{:S(2)}, u32[]{:S(2)}) collective-permute-start(f32[1,2,16384]{2,1,0:T(2,128)S(1)} %collective-permute-done.5), channel_id=1, source_target_pairs={{0,8},{8,16},{16,24},{24,0},{1,9},{9,17},{17,25},{25,1},{2,10},{10... | collective-permute-start | bytes 393224 | tf_op jit(solution)/shard_map/ppermute | solution.py:18
  155.6 9.4 %copy-start = (f32[4,2,16384]{2,1,0:T(2,128)}, f32[4,2,16384]{2,1,0:T(2,128)S(1)}, u32[]{:S(2)}) copy-start(f32[4,2,16384]{2,1,0:T(2,128)S(1)} %gather_fusion) | copy-start | bytes 1572868
Sparse Core Ops, SparseCore 0:
  12.9 70.8 all-reduce.2
